TPU v7x, 32 devices: a whole 2x2x4 slice. The times are simulated.
32 devices in a mesh: dp: 8 (over z, x), head: 4 (over y, core).
Axes of the slice: x: 2, y: 2, z: 4, core: 2. Of those that a mesh axis runs over, the one named last changes fastest.
Arguments:
- layer_input: bfloat16 [64, 197, 768], P(('dp', 'head')), may hold values from -6 to 6
- prompts: bfloat16 [100, 768], replicated, may hold values from -6 to 6
- lengths: int32 [64], P('dp'), may hold values from 1 to 100, as said below
- key_mask: int32 [64, 297], P('dp'), may hold values 0 or 1
- ln1_gain: float32 [768], replicated, may hold values from 0.1 to 1.9
- ln1_shift: float32 [768], replicated, may hold values from -1.5 to 1.5
- w_qkv: bfloat16 [3, 768, 768], P(None, 'dp', 'head'), may hold values from -0.3125 to 0.3125
- w_out: bfloat16 [768, 768], P('head', 'dp'), may hold values from -0.875 to 0.875
- b_out: float32 [768], replicated, may hold values from -1.5 to 1.5
- ln2_gain: float32 [768], replicated, may hold values from 0.1 to 1.9
- ln2_shift: float32 [768], replicated, may hold values from -1.5 to 1.5
- w_fc1: bfloat16 [768, 3072], P('dp', 'head'), may hold values from -0.21875 to 0.21875
- b_fc1: float32 [3072], P('head'), may hold values from -2.5 to 2.5
- w_fc2: bfloat16 [3072, 768], P('head', 'dp'), may hold values from -0.15625 to 0.15625
- b_fc2: float32 [768], replicated, may hold values from -1.5 to 1.5
- grad_output: bfloat16 [64, 297, 768], P(('dp', 'head')), may hold values from -6 to 6
Outputs:
- layer_output: bfloat16 [64, 297, 768], P(('dp', 'head'))
- grad_input: bfloat16 [64, 197, 768], P(('dp', 'head'))
- grad_prompts: float32 [100, 768], replicated
Inputs may be any that keep to these rules, and one draw needn't show every extreme that they name: `lengths`: each length is one of 1, 10, 50 and 100; both 1 and 100 occur.
All inputs are finite; a program needn't handle non-finite values. No bound on the sum of `key_mask` on one device may be relied on, other than what follows from the above.
Results may differ from a plain program's by a relative error of at most 0.019.
Values may be sent and summed in bfloat16 or wider, within the bound.
No kernel may reach another device: no remote copies, remote signals or barrier semaphores. Data moves between devices by JAX's collectives and lax.ppermute only.
A program may use at most 128 MiB of HBM per device.

v0:
```python
import jax
import jax.numpy as jnp
from jax import lax
from jax.sharding import PartitionSpec as P

HEAD_DIM = 64
IMG_TOK = 197
PROMPTS = 100
EPSILON = 1e-06


def layer_norm(rows, gain, shift):
    center = rows - jnp.mean(rows, axis=-1, keepdims=True)
    return (
        center * lax.rsqrt(jnp.mean(center * center, axis=-1, keepdims=True) + EPSILON) * gain
        + shift
    )


def token_masks(lengths, key_mask):
    position = lax.broadcasted_iota(jnp.int32, key_mask.shape, 1)
    used = (position < IMG_TOK) | (position - IMG_TOK < lengths[:, None])
    seen = (key_mask == 1) | (position == 0)
    return (used, used & seen)


def project(rows_b, weight):
    return jnp.einsum("isd,dc->isc", rows_b, weight, preferred_element_type=jnp.float32)


def attend(rows_b, full_qkv, visible):
    img_count, seq_len = (rows_b.shape[0], rows_b.shape[1])
    head_count = full_qkv.shape[2] // HEAD_DIM
    projected = jnp.einsum(
        "isd,tdc->tisc", rows_b, full_qkv, preferred_element_type=jnp.float32
    ).astype(jnp.bfloat16)
    projected = projected.reshape(3, img_count, seq_len, head_count, HEAD_DIM)
    query_rows, key_rows, value_rows = (projected[0], projected[1], projected[2])
    scores = jnp.einsum(
        "ishc,ithc->ihst", query_rows, key_rows, preferred_element_type=jnp.float32
    ) * HEAD_DIM ** (-0.5)
    scores = jnp.where(visible[:, None, None, :], scores, -1000000000.0)
    attn_probs = jax.nn.softmax(scores, axis=-1)
    return (query_rows, key_rows, value_rows, attn_probs)


def mix_values(probs_b, value_rows):
    img_count, seq_len = (value_rows.shape[0], value_rows.shape[1])
    context = jnp.einsum("ihst,ithc->ishc", probs_b, value_rows, preferred_element_type=jnp.float32)
    return context.astype(jnp.bfloat16).reshape(img_count, seq_len, value_rows.shape[2] * HEAD_DIM)


def mlp_back(grad_all, pre_act, fc1_rows, fc2_rows):
    grad_active_b = jnp.einsum(
        "isd,fd->isf", grad_all, fc2_rows, preferred_element_type=jnp.float32
    ).astype(jnp.bfloat16)
    _, gelu_back = jax.vjp(lambda values_in: jax.nn.gelu(values_in, approximate=False), pre_act)
    grad_pre_b = gelu_back(grad_active_b.astype(jnp.float32))[0].astype(jnp.bfloat16)
    return jnp.einsum("isf,df->isd", grad_pre_b, fc1_rows, preferred_element_type=jnp.float32)


def attn_back(grad_all, out_rows, qkv_rows, query_rows, key_rows, value_rows, attn_probs, probs_b):
    img_count, seq_len, head_count = (value_rows.shape[0], value_rows.shape[1], value_rows.shape[2])
    local_width = head_count * HEAD_DIM
    grad_context = jnp.einsum(
        "isd,cd->isc", grad_all, out_rows, preferred_element_type=jnp.float32
    ).astype(jnp.bfloat16)
    grad_context = grad_context.reshape(img_count, seq_len, head_count, HEAD_DIM)
    grad_value = jnp.einsum(
        "ihst,ishc->ithc", probs_b, grad_context, preferred_element_type=jnp.float32
    ).astype(jnp.bfloat16)
    grad_probs = jnp.einsum(
        "ishc,ithc->ihst", grad_context, value_rows, preferred_element_type=jnp.float32
    )
    grad_scores = (
        attn_probs * (grad_probs - jnp.sum(attn_probs * grad_probs, axis=-1, keepdims=True))
    ).astype(jnp.bfloat16)
    grad_query = (
        jnp.einsum("ihst,ithc->ishc", grad_scores, key_rows, preferred_element_type=jnp.float32)
        * HEAD_DIM ** (-0.5)
    ).astype(jnp.bfloat16)
    grad_key = (
        jnp.einsum("ihst,ishc->ithc", grad_scores, query_rows, preferred_element_type=jnp.float32)
        * HEAD_DIM ** (-0.5)
    ).astype(jnp.bfloat16)
    stacked = jnp.stack([grad_query, grad_key, grad_value]).reshape(
        3, img_count, seq_len, local_width
    )
    return jnp.einsum("tisc,tdc->isd", stacked, qkv_rows, preferred_element_type=jnp.float32)


def per_device(
    layer_input,
    prompts,
    lengths,
    key_mask,
    ln1_gain,
    ln1_shift,
    w_qkv,
    w_out,
    b_out,
    ln2_gain,
    ln2_shift,
    w_fc1,
    b_fc1,
    w_fc2,
    b_fc2,
    grad_output,
):
    own_count = layer_input.shape[0]
    model_width = layer_input.shape[2]
    offset = lax.axis_index("head") * own_count
    used_all, visible = token_masks(lengths, key_mask)
    used_own = lax.dynamic_slice_in_dim(used_all, offset, own_count, 0).astype(jnp.float32)[
        ..., None
    ]
    gain_one, shift_one = (ln1_gain, ln1_shift)
    gain_two, shift_two = (ln2_gain, ln2_shift)
    full_qkv, full_out, full_fc1, full_fc2 = (
        lax.all_gather(w_qkv, "dp", axis=1, tiled=True),
        lax.all_gather(w_out, "dp", axis=1, tiled=True),
        lax.all_gather(w_fc1, "dp", axis=0, tiled=True),
        lax.all_gather(w_fc2, "dp", axis=1, tiled=True),
    )
    prompt_rows = jnp.broadcast_to(
        prompts.astype(jnp.float32)[None], (own_count, PROMPTS, model_width)
    )
    stream = jnp.concatenate([layer_input.astype(jnp.float32), prompt_rows], axis=1)
    normed_attn, back_attn_norm = jax.vjp(
        lambda rows: layer_norm(rows, gain_one, shift_one), stream
    )
    normed_attn_b = normed_attn.astype(jnp.bfloat16)
    grad_rows = grad_output.astype(jnp.float32) * used_own
    gathered_attn = lax.all_gather(normed_attn_b, "head", axis=0, tiled=True)
    query_rows, key_rows, value_rows, attn_probs = attend(gathered_attn, full_qkv, visible)
    probs_b = attn_probs.astype(jnp.bfloat16)
    context = mix_values(probs_b, value_rows)
    attn_sum = lax.psum_scatter(
        project(context, full_out).astype(jnp.bfloat16), "head", scatter_dimension=0, tiled=True
    ).astype(jnp.float32)
    hidden_mid = stream + attn_sum + b_out
    normed_mlp, back_mlp_norm = jax.vjp(
        lambda rows: layer_norm(rows, gain_two, shift_two), hidden_mid
    )
    normed_mlp_b = normed_mlp.astype(jnp.bfloat16)
    gathered_mlp = lax.all_gather(normed_mlp_b, "head", axis=0, tiled=True)
    pre_act = project(gathered_mlp, full_fc1) + b_fc1
    active_b = jax.nn.gelu(pre_act, approximate=False).astype(jnp.bfloat16)
    mlp_sum = lax.psum_scatter(
        project(active_b, full_fc2).astype(jnp.bfloat16), "head", scatter_dimension=0, tiled=True
    ).astype(jnp.float32)
    result = ((hidden_mid + mlp_sum + b_fc2) * used_own).astype(jnp.bfloat16)
    held_inputs = lax.optimization_barrier((w_qkv, w_out, w_fc1, w_fc2, grad_rows))
    grad_rows = held_inputs[4]
    back_qkv, back_out, back_fc1, back_fc2 = (
        lax.all_gather(held_inputs[0], "dp", axis=1, tiled=True),
        lax.all_gather(held_inputs[1], "dp", axis=1, tiled=True),
        lax.all_gather(held_inputs[2], "dp", axis=0, tiled=True),
        lax.all_gather(held_inputs[3], "dp", axis=1, tiled=True),
    )
    grad_mlp_b = grad_rows.astype(jnp.bfloat16)
    grad_mlp_all, gathered_again = (
        lax.all_gather(grad_mlp_b, "head", axis=0, tiled=True),
        lax.all_gather(normed_mlp_b, "head", axis=0, tiled=True),
    )
    pre_act = project(gathered_again, back_fc1) + b_fc1
    grad_normed_mlp = lax.psum_scatter(
        mlp_back(grad_mlp_all, pre_act, back_fc1, back_fc2).astype(jnp.bfloat16),
        "head",
        scatter_dimension=0,
        tiled=True,
    ).astype(jnp.float32)
    grad_mid = grad_rows + back_mlp_norm(grad_normed_mlp)[0]
    grad_attn_b = grad_mid.astype(jnp.bfloat16)
    grad_attn_all, gathered_again = (
        lax.all_gather(grad_attn_b, "head", axis=0, tiled=True),
        lax.all_gather(normed_attn_b, "head", axis=0, tiled=True),
    )
    query_rows, key_rows, value_rows, attn_probs = attend(gathered_again, back_qkv, visible)
    probs_b = attn_probs.astype(jnp.bfloat16)
    grad_partial = attn_back(
        grad_attn_all, back_out, back_qkv, query_rows, key_rows, value_rows, attn_probs, probs_b
    )
    grad_normed_attn = lax.psum_scatter(
        grad_partial.astype(jnp.bfloat16), "head", scatter_dimension=0, tiled=True
    ).astype(jnp.float32)
    grad_stream = grad_mid + back_attn_norm(grad_normed_attn)[0]
    grad_input = grad_stream[:, :IMG_TOK].astype(jnp.bfloat16)
    grad_prompts = lax.psum(jnp.sum(grad_stream[:, IMG_TOK:], axis=0), ("dp", "head"))
    return (result, grad_input, grad_prompts)


def solution(mesh):
    placed = (
        P(("dp", "head"), None, None),
        P(),
        P("dp"),
        P("dp", None),
        P(),
        P(),
        P(None, "dp", "head"),
        P("head", "dp"),
        P(),
        P(),
        P(),
        P("dp", "head"),
        P("head"),
        P("head", "dp"),
        P(),
        P(("dp", "head"), None, None),
    )
    return jax.shard_map(
        per_device,
        mesh=mesh,
        in_specs=placed,
        out_specs=(P(("dp", "head"), None, None), P(("dp", "head"), None, None), P()),
        check_vma=False,
    )
```

profile of v0, /device:TPU:8, one launch (start us, length us, event | category | flops | bytes accessed | tf_op | source)
XLA Modules:
  0.0 717.3 jit_solution(3644398181313778874)
XLA Ops:
  10.9 1.3 add_convert_fusion.1
  12.6 36.7 %all_gather.39 = bf16[3,768,192]{2,0,1:T(4,128)(2,1)} all-gather(bf16[3,96,192]{2,0,1:T(4,128)(2,1)S(1)} %copy.34), channel_id=1, replica_groups=mesh['dp'=8,'head'=4] {'dp'}, dimensions={1}, use_global_device_ids=true | all-gather | bytes 995328 | tf_op jit(solution)/shard_map/all_gather | solution.py:120
  49.3 3.4 copy.35
  52.7 30.5 %all_gather.40 = bf16[192,768]{0,1:T(8,128)(2,1)S(1)} all-gather(bf16[192,96]{0,1:T(8,128)(2,1)S(1)} %copy.37), channel_id=1, replica_groups=mesh['dp'=8,'head'=4] {'dp'}, dimensions={1}, use_global_device_ids=true | all-gather | bytes 331776 | tf_op jit(solution)/shard_map/all_gather | solution.py:121
  83.3 5.2 convert_bitcast_fusion.1
  88.6 1.9 fusion.167
  90.5 8.2 %fusion.168 = (f32[8,3,297]{2,1,0:T(4,128)S(1)}, f32[8,3,297,297]{2,3,1,0:T(8,128)}) fusion(pred[8,297]{1,0:T(8,128)(4,1)S(1)} %get-tuple-element.30, bf16[8,297,3,64]{1,3,2,0:T(8,128)(2,1)} %bitcast.105, bf16[8,297,3,64]{1,3,2,0:T(8,128)(2,1)} %bitcast.104), kind=kOutput, calls=%fused_computation.222 | convolution fusion | flops 279446432 | bytes 10323720 | tf_op jit(solution)/shard_map/sub | solution.py:43
  98.7 5.8 fusion.73
  104.4 3.2 convolution_convert_fusion
  108.8 1.5 convert_multiply_fusion.4
  110.4 41.4 %reduce-scatter.5.cloned.1.call-done = bf16[2,297,768]{2,1,0:T(8,128)(2,1)} async-done(((bf16[8,297,768]{2,1,0:T(8,128)(2,1)}), bf16[2,297,768]{2,1,0:T(8,128)(2,1)}) %reduce-scatter.5.cloned.1.call-update) | async-done | bytes 912400 | tf_op jit(solution)/shard_map/reduce_scatter | solution.py:138
  151.8 1.6 fusion.165
  153.4 1.7 multiply_reduce_fusion.3
  155.1 1.5 add_convert_fusion
  157.3 2.6 convert_element_type.129
  161.7 26.8 %all-gather.11.cloned.1.call-done = bf16[8,297,768]{2,1,0:T(8,128)(2,1)} async-done(((bf16[2,297,768]{2,1,0:T(8,128)(2,1)}), bf16[8,297,768]{2,1,0:T(8,128)(2,1)}) %all-gather.11.cloned.1.call-update) | async-done | bytes 3649552 | tf_op jit(solution)/shard_map/all_gather | solution.py:146
  188.5 8.4 %fusion.82 = f32[8,297,768]{2,1,0:T(8,128)} fusion(bf16[8,297,768]{2,1,0:T(8,128)(2,1)} %all-gather.11.cloned.1.call-done, bf16[768,768]{1,0:T(8,128)(2,1)} %all-gather.17.cloned.1.call-done), kind=kOutput, calls=%fused_computation.120 | convolution fusion | flops 2802843648 | bytes 12128256 | tf_op jit(solution)/shard_map/isd,dc->isc/dot_general | solution.py:28
  196.9 34.4 %all-gather.21.cloned.1.call-done = bf16[768,768]{0,1:T(8,128)(2,1)} async-done(((bf16[768,96]{0,1:T(8,128)(2,1)}), bf16[768,768]{0,1:T(8,128)(2,1)}) %all-gather.21.cloned.1.call-update) | async-done | bytes 1179664 | tf_op jit(solution)/shard_map/all_gather | solution.py:159
  231.3 32.9 %all-gather.19.cloned.1.call-done = bf16[8,297,768]{2,1,0:T(8,128)(2,1)} async-done(((bf16[2,297,768]{2,1,0:T(8,128)(2,1)}), bf16[8,297,768]{2,1,0:T(8,128)(2,1)}) %all-gather.19.cloned.1.call-update) | async-done | bytes 3649552 | tf_op jit(solution)/shard_map/all_gather | solution.py:163
  264.2 27.0 %fusion.57 = bf16[8,297,768]{2,1,0:T(8,128)(2,1)} fusion(f32[8,297,768]{2,1,0:T(8,128)} %fusion.82, f32[768]{0:T(1024)S(1)} %copy-done.35, bf16[8,297,768]{2,1,0:T(8,128)(2,1)} %all-gather.19.cloned.1.call-done, bf16[768,768]{0,1:T(8,128)(2,1)} %all-gather.21.cloned.1.call-done, bf16[768,768]{1,0:T(8,128)(2,1)} %all-gather.17.cloned.1.call-done), kind=kOutput, calls=%fused_computation.89 | convolution fusion | flops 5744369664 | bytes 16960512 | tf_op jit(solution)/shard_map/isf,df->isd/dot_general | solution.py:59
  291.2 9.2 %reduce-scatter.7.cloned.1.call-start = ((), (), s32[]{:S(2)}) async-start(), calls=%async_computation.9 | async-start | bytes 4669440 | tf_op jit(solution)/shard_map/reduce_scatter | solution.py:149
  300.4 6.6 all-gather.13.cloned.1.call-done
  307.0 10.3 %fusion.70 = (u8[297,768]{1,0:T(8,128)(4,1)S(1)}, u8[297,768]{1,0:T(8,128)(4,1)S(1)}, f32[8,297,768]{2,1,0:T(8,128)}) fusion(f32[768]{0:T(1024)S(1)} %copy-done.35, bf16[8,297,768]{2,1,0:T(8,128)(2,1)} %all-gather.11.cloned.1.call-done, bf16[768,768]{1,0:T(8,128)(2,1)} %all-gather.13.cloned.1.call-done), kind=kOutput, calls=%fused_computation.109 | convolution fusion | flops 2827934208 | bytes 12587520 | tf_op jit(solution)/shard_map/isd,dc->isc/dot_general | solution.py:28
  317.2 32.0 %all-gather.15.cloned.1.call-done = bf16[768,768]{0,1:T(8,128)(2,1)} async-done(((bf16[768,96]{0,1:T(8,128)(2,1)}), bf16[768,768]{0,1:T(8,128)(2,1)}) %all-gather.15.cloned.1.call-update) | async-done | bytes 1179664 | tf_op jit(solution)/shard_map/all_gather | solution.py:123
  349.3 23.0 %fusion.60 = bf16[8,297,768]{2,1,0:T(8,128)(2,1)} fusion(f32[8,297,768]{2,1,0:T(8,128)} %get-tuple-element.33, f32[768]{0:T(1024)S(1)} %copy-done.35, bf16[768,768]{0,1:T(8,128)(2,1)} %all-gather.15.cloned.1.call-done, u8[297,768]{1,0:T(8,128)(4,1)S(1)} %get-tuple-element.20, u8[297,768]{1,0:T(8,128)(4,1)S(1)} %get-tuple-element.19), kind=kOutput, calls=%fused_computation.90 | convolution fusion | flops 2934226944 | bytes 12587520 | tf_op jit(solution)/shard_map/isd,dc->isc/dot_general | solution.py:28
  372.4 1.9 multiply_reduce_fusion.2
  375.4 38.2 %reduce-scatter.7.cloned.1.call-done = bf16[2,297,768]{2,1,0:T(8,128)(2,1)} async-done(((bf16[8,297,768]{2,1,0:T(8,128)(2,1)}), bf16[2,297,768]{2,1,0:T(8,128)(2,1)}) %reduce-scatter.7.cloned.1.call-update) | async-done | bytes 912400 | tf_op jit(solution)/shard_map/reduce_scatter | solution.py:149
  413.6 3.6 fusion.164
  417.5 28.5 %all_gather.49 = bf16[192,768]{0,1:T(8,128)(2,1)S(1)} all-gather(bf16[192,96]{0,1:T(8,128)(2,1)S(1)} %copy.42), channel_id=1, replica_groups=mesh['dp'=8,'head'=4] {'dp'}, dimensions={1}, use_global_device_ids=true | all-gather | bytes 331776 | tf_op jit(solution)/shard_map/all_gather | solution.py:157
  446.1 39.4 %all_gather.47 = bf16[3,768,192]{2,0,1:T(4,128)(2,1)S(1)} all-gather(bf16[3,96,192]{2,0,1:T(4,128)(2,1)S(1)} %copy.40), channel_id=1, replica_groups=mesh['dp'=8,'head'=4] {'dp'}, dimensions={1}, use_global_device_ids=true | all-gather | bytes 995328 | tf_op jit(solution)/shard_map/all_gather | solution.py:156
  485.5 7.7 %convert_bitcast_fusion = bf16[3,8,297,192]{2,3,1,0:T(8,128)(2,1)S(1)} fusion(bf16[8,297,768]{2,1,0:T(8,128)(2,1)} %all-gather.9.cloned.1.call-done, bf16[3,768,192,1]{2,0,1,3:T(4,128)(2,1)S(1)} %bitcast.101), kind=kOutput, calls=%fused_computation.84 | convolution fusion | flops 2103501312 | bytes 7271424 | tf_op jit(solution)/shard_map/isd,tdc->tisc/dot_general | solution.py:34
  493.2 2.0 fusion.166
  495.2 8.2 %fusion.169 = (f32[8,3,297]{2,1,0:T(4,128)S(1)}, f32[8,3,297,297]{2,3,1,0:T(8,128)}) fusion(pred[8,297]{1,0:T(8,128)(4,1)S(1)} %copy-done.33, bf16[8,297,3,64]{1,3,2,0:T(8,128)(2,1)} %bitcast.98, bf16[8,297,3,64]{1,3,2,0:T(8,128)(2,1)} %bitcast.96), kind=kOutput, calls=%fused_computation.223 | convolution fusion | flops 279446432 | bytes 10323720 | tf_op jit(solution)/shard_map/sub | solution.py:43
  503.5 3.6 convolution_convert_fusion.1
  507.1 7.6 %fusion.74 = bf16[8,3,64,297]{3,2,1,0:T(8,128)(2,1)} fusion(bf16[8,297,3,64]{1,3,2,0:T(8,128)(2,1)S(1)} %bitcast.109, f32[8,3,297,297]{2,3,1,0:T(8,128)} %get-tuple-element.35, f32[8,3,297]{2,1,0:T(4,128)S(1)} %get-tuple-element.34), kind=kOutput, calls=%fused_computation.113 | convolution fusion | flops 275668288 | bytes 10321344 | tf_op jit(solution)/shard_map/ihst,ishc->ithc/dot_general | solution.py:69
  514.8 3.4 multiply_reduce_fusion
  518.2 1.7 multiply_convert_fusion
  519.9 3.3 multiply_convert_fusion.1
  525.0 5.4 bitcast_convert_fusion
  530.5 42.3 %reduce-scatter.11.cloned.1.call-done = bf16[2,297,768]{2,1,0:T(8,128)(2,1)} async-done(((bf16[8,297,768]{2,1,0:T(8,128)(2,1)}), bf16[2,297,768]{2,1,0:T(8,128)(2,1)}) %reduce-scatter.11.cloned.1.call-update) | async-done | bytes 912400 | tf_op jit(solution)/shard_map/reduce_scatter | solution.py:184
  572.8 1.8 multiply_reduce_fusion.1
  574.7 1.9 fusion.92
  576.6 1.6 add_add_fusion.2
  580.4 2.8 copy.51
  583.2 1.3 slice.49
  584.5 1.3 copy.52
  585.8 122.2 %all-reduce.2.cloned.1.call-done = f32[100,768]{1,0:T(8,128)} async-done(((f32[100,768]{1,0:T(8,128)}), f32[100,768]{1,0:T(8,128)}) %all-reduce.2.cloned.1.call-update) | async-done | bytes 307216 | tf_op jit(solution)/shard_map/psum | solution.py:189
  708.1 1.7 copy.75
  (135 shorter events, 12.2 us)
Async XLA Ops:
  8.0 2.8 copy-start.18
  8.0 2.8 copy-start.29
  8.0 75.3 %all-gather.9.cloned.1.call-start = ((), (), s32[]{:S(2)}) async-start(), calls=%async_computation.4 | async-start | bytes 4669440 | tf_op jit(solution)/shard_map/all_gather | solution.py:134
  10.2 2.1 copy-start.13
  10.2 2.2 copy-start.10
  10.4 1.9 copy-start.15
  12.2 71.0 %copy-start.28 = (s32[8,297]{1,0:T(8,128)S(1)}, s32[8,297]{1,0:T(8,128)}, u32[]{:S(2)}) copy-start(s32[8,297]{1,0:T(8,128)} %param.19) | copy-start | bytes 28516
  12.2 71.0 %copy-start.34 = (s32[8]{0:T(128)S(1)}, s32[8]{0:T(128)}, u32[]{:S(2)}) copy-start(s32[8]{0:T(128)} %param.18) | copy-start | bytes 100
  12.2 139.5 %reduce-scatter.5.cloned.1.call-start = ((), (), s32[]{:S(2)}) async-start(), calls=%async_computation.5 | async-start | bytes 4669440 | tf_op jit(solution)/shard_map/reduce_scatter | solution.py:138
  83.3 7.2 copy-start.32
  107.7 44.1 %copy-start.12 = (f32[768]{0:T(1024)S(1)}, f32[768]{0:T(1024)}, u32[]{:S(2)}) copy-start(f32[768]{0:T(1024)} %param.24) | copy-start | bytes 9220
  107.7 54.0 %all-gather.17.cloned.1.call-start = ((), (), s32[]{:S(2)}) async-start(), calls=%async_computation.10 | async-start | bytes 1327104 | tf_op jit(solution)/shard_map/all_gather | solution.py:158
  110.3 44.8 %copy-start.17 = (f32[768]{0:T(1024)S(1)}, f32[768]{0:T(1024)}, u32[]{:S(2)}) copy-start(f32[768]{0:T(1024)} %param.25) | copy-start | bytes 9220
  110.3 44.8 %copy-start.30 = (f32[768]{0:T(1024)S(1)}, f32[768]{0:T(1024)}, u32[]{:S(2)}) copy-start(f32[768]{0:T(1024)} %param.26) | copy-start | bytes 9220
  110.3 78.1 %all-gather.11.cloned.1.call-start = ((), (), s32[]{:S(2)}) async-start(), calls=%async_computation.6 | async-start | bytes 4669440 | tf_op jit(solution)/shard_map/all_gather | solution.py:146
  151.8 3.4 copy-start
  155.1 4.7 copy-start.26
  156.6 74.7 %all-gather.21.cloned.1.call-start = ((), (), s32[]{:S(2)}) async-start(), calls=%async_computation.12 | async-start | bytes 1327104 | tf_op jit(solution)/shard_map/all_gather | solution.py:159
  157.2 107.0 %all-gather.19.cloned.1.call-start = ((), (), s32[]{:S(2)}) async-start(), calls=%async_computation.11 | async-start | bytes 4669440 | tf_op jit(solution)/shard_map/all_gather | solution.py:163
  159.9 147.1 %all-gather.13.cloned.1.call-start = ((), (), s32[]{:S(2)}) async-start(), calls=%async_computation.7 | async-start | bytes 1327104 | tf_op jit(solution)/shard_map/all_gather | solution.py:122
  160.6 188.6 %all-gather.15.cloned.1.call-start = ((), (), s32[]{:S(2)}) async-start(), calls=%async_computation.8 | async-start | bytes 1327104 | tf_op jit(solution)/shard_map/all_gather | solution.py:123
  161.4 102.9 %copy-start.35 = (f32[768]{0:T(1024)S(1)}, f32[768]{0:T(1024)}, u32[]{:S(2)}) copy-start(f32[768]{0:T(1024)} %param.28) | copy-start | bytes 9220
  161.4 211.0 %reduce-scatter.9.cloned.1.call-start = ((), (), s32[]{:S(2)}) async-start(), calls=%async_computation.13 | async-start | bytes 4669440 | tf_op jit(solution)/shard_map/reduce_scatter | solution.py:167
  291.2 122.4 %reduce-scatter.7.cloned.1.call-start = ((), (), s32[]{:S(2)}) async-start(), calls=%async_computation.9 | async-start | bytes 4669440 | tf_op jit(solution)/shard_map/reduce_scatter | solution.py:149
  372.3 2.1 copy-start.27
  372.3 41.3 %copy-start.23 = (f32[2,297]{1,0:T(2,128)S(1)}, f32[2,297]{1,0:T(2,128)}, u32[]{:S(2)}) copy-start(f32[2,297]{1,0:T(2,128)} %copy-done.22) | copy-start | bytes 7132
  372.3 41.3 %copy-start.31 = (f32[768]{0:T(1024)S(1)}, f32[768]{0:T(1024)}, u32[]{:S(2)}) copy-start(f32[768]{0:T(1024)} %param.30) | copy-start | bytes 9220
  372.3 131.1 %all-gather.23.cloned.1.call-start = ((), (), s32[]{:S(2)}) async-start(), calls=%async_computation.14 | async-start | bytes 4669440 | tf_op jit(solution)/shard_map/all_gather | solution.py:176
  372.4 2.0 copy-start.2
  375.4 41.9 %copy-start.14 = (bf16[192,96]{1,0:T(8,128)(2,1)S(1)}, bf16[192,96]{1,0:T(8,128)(2,1)}, u32[]{:S(2)}) copy-start(bf16[192,96]{1,0:T(8,128)(2,1)} %param.23) | copy-start | bytes 110596
  375.4 42.0 %copy-start.11 = (bf16[3,96,192]{2,1,0:T(8,128)(2,1)S(1)}, bf16[3,96,192]{2,1,0:T(8,128)(2,1)}, u32[]{:S(2)}) copy-start(bf16[3,96,192]{2,1,0:T(8,128)(2,1)} %param.22) | copy-start | bytes 331780
  417.2 155.5 %reduce-scatter.11.cloned.1.call-start = ((), (), s32[]{:S(2)}) async-start(), calls=%async_computation.15 | async-start | bytes 4669440 | tf_op jit(solution)/shard_map/reduce_scatter | solution.py:184
  485.5 7.7 %copy-start.7 = (bf16[3,768,192]{2,0,1:T(4,128)(2,1)}, bf16[3,768,192]{2,0,1:T(4,128)(2,1)S(1)}, u32[]{:S(2)}) copy-start(bf16[3,768,192]{2,0,1:T(4,128)(2,1)S(1)} %all_gather.47) | copy-start | bytes 2654212
  493.2 2.0 copy-start.33
  503.5 11.3 %slice-start = ((s8[11206656]{0:T(1024)(128)(4,1)}), s8[4194304]{0:T(1024)(128)(4,1)S(1)}, s32[]{:S(2)}) async-start(s8[11206656]{0:T(1024)(128)(4,1)} %bitcast.94), calls=%async_computation.17 | async-start | bytes 8388608
  507.1 7.7 %copy-start.37 = (bf16[8,297,192]{1,2,0:T(8,128)(2,1)}, bf16[8,297,192]{1,2,0:T(8,128)(2,1)S(1)}, u32[]{:S(2)}) copy-start(bf16[8,297,192]{1,2,0:T(8,128)(2,1)S(1)} %convolution_convert_fusion.1) | copy-start | bytes 2737156
  507.1 7.7 %slice-start.1 = ((s8[11206656]{0:T(1024)(128)(4,1)}), s8[4194304]{0:T(1024)(128)(4,1)S(1)}, s32[]{:S(2)}) async-start(s8[11206656]{0:T(1024)(128)(4,1)} %bitcast.94), calls=%async_computation.18 | async-start | bytes 8388608
  507.1 7.7 %slice-start.2 = ((s8[11206656]{0:T(1024)(128)(4,1)}), s8[2818048]{0:T(1024)(128)(4,1)S(1)}, s32[]{:S(2)}) async-start(s8[11206656]{0:T(1024)(128)(4,1)} %bitcast.94), calls=%async_computation.19 | async-start | bytes 5636096
  519.9 3.3 copy-start.5
  523.2 1.7 copy-start.36
  530.4 42.4 %copy-start.16 = (f32[2,297]{1,0:T(2,128)S(1)}, f32[2,297]{1,0:T(2,128)}, u32[]{:S(2)}) copy-start(f32[2,297]{1,0:T(2,128)} %copy-done.15) | copy-start | bytes 7132
  530.4 42.4 %copy-start.19 = (f32[768]{0:T(1024)S(1)}, f32[768]{0:T(1024)}, u32[]{:S(2)}) copy-start(f32[768]{0:T(1024)} %param.20) | copy-start | bytes 9220
  530.4 44.2 %copy-start.25 = (f32[2,297]{1,0:T(2,128)S(1)}, f32[2,297]{1,0:T(2,128)}, u32[]{:S(2)}) copy-start(f32[2,297]{1,0:T(2,128)} %copy-done.24) | copy-start | bytes 7132
  530.4 44.2 %copy-start.21 = (f32[2,297]{1,0:T(2,128)S(1)}, f32[2,297]{1,0:T(2,128)}, u32[]{:S(2)}) copy-start(f32[2,297]{1,0:T(2,128)} %copy-done.20) | copy-start | bytes 7132
  530.4 177.6 %all-reduce.2.cloned.1.call-start = ((), (), s32[]{:S(2)}) async-start(), calls=%async_computation.16 | async-start | bytes 638976 | tf_op jit(solution)/shard_map/psum | solution.py:189
  572.8 3.8 copy-start.1
  572.8 3.8 copy-start.3
  572.8 3.9 copy-start.4
  (6 other events, 8.3 us)
Sparse Core Ops, SparseCore 0:
  12.4 33.0 all-gather.8
  107.8 43.8 reduce-scatter.4
  291.3 41.6 reduce-scatter.8
  372.4 41.1 reduce-scatter.6
  580.5 127.5 all-reduce.1
Sparse Core Ops, SparseCore 1:
  110.6 42.7 all-gather.16
  156.7 31.7 all-gather.10
  190.8 40.5 all-gather.20
  233.0 31.2 all-gather.18
  266.4 40.5 all-gather.12
  309.2 40.0 all-gather.14
  417.3 31.7 all-gather.22
  530.5 42.2 reduce-scatter.10
where the time goes:
time: 726 us; the launch traced here: 717 us
  waiting for transfers between devices  379 us (52%)
  blocking collectives  135 us (19%)
  matrix products  132 us (18%)
  other arithmetic  26.4 us (4%)
  local copies, waits for them, and re-layouts  18.9 us (3%)
  between operations  16.4 us (2%)
  starting transfers between devices  9.95 us (1%)
    psum x1, waiting for transfers between devices, per_device(): lax.psum(jnp.sum(grad_stream[:, IMG_TOK:], axis=0), ('dp', 'head'))  122 us
    dot_general x4, matrix products, project(): jnp.einsum('isd,dc->isc', rows_b, weight, preferred_element_type=jnp.floa...  44.9 us
    reduce_scatter x1, waiting for transfers between devices, per_device(): lax.psum_scatter(grad_partial.astype(jnp.bfloat16), 'head', scatter_dimen...  42.3 us
    reduce_scatter x1, waiting for transfers between devices, per_device(): lax.psum_scatter(project(context, full_out).astype(jnp.bfloat16), 'head',...  41.4 us
    all_gather x1, blocking collectives, per_device(): lax.all_gather(held_inputs[0], 'dp', axis=1, tiled=True)  39.4 us
    reduce_scatter x1, waiting for transfers between devices, per_device(): lax.psum_scatter(project(active_b, full_fc2).astype(jnp.bfloat16), 'head'...  38.2 us
    all_gather x1, blocking collectives, per_device(): lax.all_gather(w_qkv, 'dp', axis=1, tiled=True)  36.7 us
    all_gather x1, waiting for transfers between devices, per_device(): lax.all_gather(held_inputs[3], 'dp', axis=1, tiled=True)  34.4 us
  transfers between devices with their start and end apart: 13, of which 9 were waited for; matrix products, arithmetic and copies ran while one was open for 15% of the time, Pallas kernels for 0%

commit v1 on v0

--- a/solution.py
+++ b/solution.py
@@ -7,6 +7,27 @@
 IMG_TOK = 197
 PROMPTS = 100
 EPSILON = 1e-06
+
+
+def gather_around(shard, axis, dim):
+    size, index, width = (lax.axis_size(axis), lax.axis_index(axis), shard.shape[dim])
+    right = [(i, (i + 1) % size) for i in range(size)]
+    downward = [(i, (i - 1) % size) for i in range(size)]
+    whole = jnp.zeros((*shard.shape[:dim], size * width, *shard.shape[dim + 1 :]), shard.dtype)
+    whole = lax.dynamic_update_slice_in_dim(whole, shard, index * width, axis=dim)
+    from_left = from_right = shard
+    half = size // 2
+    for lap in range(1, half + 1):
+        from_left = lax.ppermute(from_left, axis, right)
+        whole = lax.dynamic_update_slice_in_dim(
+            whole, from_left, (index - lap) % size * width, axis=dim
+        )
+        if lap < size - half:
+            from_right = lax.ppermute(from_right, axis, downward)
+            whole = lax.dynamic_update_slice_in_dim(
+                whole, from_right, (index + lap) % size * width, axis=dim
+            )
+    return whole
 
 
 def layer_norm(rows, gain, shift):
@@ -156,7 +177,7 @@
         lax.all_gather(held_inputs[0], "dp", axis=1, tiled=True),
         lax.all_gather(held_inputs[1], "dp", axis=1, tiled=True),
         lax.all_gather(held_inputs[2], "dp", axis=0, tiled=True),
-        lax.all_gather(held_inputs[3], "dp", axis=1, tiled=True),
+        gather_around(held_inputs[3], "dp", 1),
     )
     grad_mlp_b = grad_rows.astype(jnp.bfloat16)
     grad_mlp_all, gathered_again = (

time: 726 us -> 686 us (0.945)
  waiting for transfers between devices: 379 us -> 311 us
  local copies, waits for them, and re-layouts: 18.9 us -> 43 us
    all_gather x1 -> x0, waiting for transfers between devices: 34.4 us -> none  [per_device(): lax.all_gather(held_inputs[3], 'dp', axis=1, tiled=True)]
    all_gather x1, waiting for transfers between devices: 32.9 us -> 1.03 us  [per_device(): lax.all_gather(grad_mlp_b, 'head', axis=0, tiled=True)]
    all_gather x1, waiting for transfers between devices: 26.8 us -> 0.03 us  [per_device(): gathered_mlp = lax.all_gather(normed_mlp_b, 'head', axis=0, tiled=True)]
    dynamic_update_slice x0 -> x8, local copies, waits for them, and re-layouts: none -> 20.8 us  [the longest x4 10.2 us: gather_around(): lax.dynamic_update_slice_in_dim(whole, from_left, (index - lap) % size *...]
    ppermute x0 -> x7, waiting for transfers between devices: none -> 18.1 us  [the longest x4 18 us: gather_around(): from_left = lax.ppermute(from_left, axis, right)]
    ppermute x0 -> x7, starting transfers between devices: none -> 11.4 us  [the longest x4 8.96 us: gather_around(): from_left = lax.ppermute(from_left, axis, right)]
    all_gather x1, waiting for transfers between devices: 6.59 us -> 15.8 us  [per_device(): lax.all_gather(w_fc1, 'dp', axis=0, tiled=True)]
    reduce_scatter x1, starting transfers between devices: 9.19 us -> 0.21 us  [per_device(): lax.psum_scatter(project(active_b, full_fc2).astype(jnp.bfloat16), 'head'...]
  transfers between devices with their start and end apart: 13 -> 19, of which waited for: 9 -> 11; matrix products, arithmetic and copies ran while one was open for 15% -> 19% of each run, Pallas kernels for 0% -> 0%
where the time goes in v1:
time: 686 us; the launch traced here: 677 us
  waiting for transfers between devices  311 us (45%)
  blocking collectives  134 us (20%)
  matrix products  130 us (19%)
  local copies, waits for them, and re-layouts  43 us (6%)
  other arithmetic  30.6 us (4%)
  between operations  16.8 us (2%)
  starting transfers between devices  12.1 us (2%)
    psum x1, waiting for transfers between devices, per_device(): lax.psum(jnp.sum(grad_stream[:, IMG_TOK:], axis=0), ('dp', 'head'))  122 us
    dot_general x4, matrix products, project(): jnp.einsum('isd,dc->isc', rows_b, weight, preferred_element_type=jnp.floa...  45 us
    reduce_scatter x1, waiting for transfers between devices, per_device(): lax.psum_scatter(grad_partial.astype(jnp.bfloat16), 'head', scatter_dimen...  42.3 us
    reduce_scatter x1, waiting for transfers between devices, per_device(): lax.psum_scatter(project(context, full_out).astype(jnp.bfloat16), 'head',...  41.8 us
    all_gather x1, blocking collectives, per_device(): lax.all_gather(held_inputs[0], 'dp', axis=1, tiled=True)  39.4 us
    reduce_scatter x1, waiting for transfers between devices, per_device(): lax.psum_scatter(project(active_b, full_fc2).astype(jnp.bfloat16), 'head'...  36.7 us
    all_gather x1, blocking collectives, per_device(): lax.all_gather(w_qkv, 'dp', axis=1, tiled=True)  35.2 us
    all_gather x1, waiting for transfers between devices, per_device(): lax.all_gather(w_fc2, 'dp', axis=1, tiled=True)  31.8 us
  transfers between devices with their start and end apart: 19, of which 11 were waited for; matrix products, arithmetic and copies ran while one was open for 19% of the time, Pallas kernels for 0%

profile of v1, /device:TPU:8, one launch (start us, length us, event | category | flops | bytes accessed | tf_op | source)
XLA Modules:
  0.0 677.0 jit_solution(2125102141788743920)
XLA Ops:
  13.9 35.2 %all_gather.36 = bf16[3,768,192]{2,0,1:T(4,128)(2,1)S(1)} all-gather(bf16[3,96,192]{2,0,1:T(4,128)(2,1)S(1)} %copy.42), channel_id=1, replica_groups=mesh['dp'=8,'head'=4] {'dp'}, dimensions={1}, use_global_device_ids=true | all-gather | bytes 995328 | tf_op jit(solution)/shard_map/all_gather | solution.py:141
  49.1 2.0 copy.43
  51.1 30.5 %all_gather.37 = bf16[192,768]{0,1:T(8,128)(2,1)S(1)} all-gather(bf16[192,96]{0,1:T(8,128)(2,1)S(1)} %copy.45), channel_id=1, replica_groups=mesh['dp'=8,'head'=4] {'dp'}, dimensions={1}, use_global_device_ids=true | all-gather | bytes 331776 | tf_op jit(solution)/shard_map/all_gather | solution.py:142
  81.7 5.2 convert_bitcast_fusion.1
  87.0 1.9 fusion.167
  88.8 8.1 %fusion.168 = (f32[8,3,297]{2,1,0:T(4,128)S(1)}, f32[8,3,297,297]{2,3,1,0:T(8,128)}) fusion(pred[8,297]{1,0:T(8,128)(4,1)S(1)} %get-tuple-element.30, bf16[8,297,3,64]{1,3,2,0:T(8,128)(2,1)} %bitcast.105, bf16[8,297,3,64]{1,3,2,0:T(8,128)(2,1)} %bitcast.104), kind=kOutput, calls=%fused_computation.222 | convolution fusion | flops 279446432 | bytes 10323720 | tf_op jit(solution)/shard_map/sub | solution.py:64
  97.0 5.4 fusion.73
  102.4 3.3 convolution_convert_fusion
  107.9 41.8 %reduce-scatter.5.cloned.1.call-done = bf16[2,297,768]{2,1,0:T(8,128)(2,1)} async-done(((bf16[8,297,768]{2,1,0:T(8,128)(2,1)}), bf16[2,297,768]{2,1,0:T(8,128)(2,1)}) %reduce-scatter.5.cloned.1.call-update) | async-done | bytes 912400 | tf_op jit(solution)/shard_map/reduce_scatter | solution.py:159
  155.9 2.6 convert_element_type.129
  162.3 5.7 collective-permute-done
  168.0 2.5 collective-permute-start.2
  171.1 5.9 collective-permute-done.2
  177.1 2.5 collective-permute-start.4
  180.0 6.3 collective-permute-done.4
  186.3 2.5 collective-permute-start.6
  189.3 2.9 dynamic_update_slice.24
  192.3 2.9 dynamic_update_slice.25
  195.3 2.9 dynamic_update_slice.26
  198.4 2.0 dynamic_update_slice.27
  200.6 2.0 dynamic_update_slice.28
  202.8 2.4 dynamic_update_slice.29
  205.4 2.9 dynamic_update_slice.30
  208.4 2.9 dynamic_update_slice.31
  211.4 8.5 %fusion.82 = f32[8,297,768]{2,1,0:T(8,128)} fusion(bf16[8,297,768]{2,1,0:T(8,128)(2,1)} %all-gather.10.cloned.1.call-done, bf16[768,768]{1,0:T(8,128)(2,1)} %all-gather.16.cloned.1.call-done), kind=kOutput, calls=%fused_computation.120 | convolution fusion | flops 2802843648 | bytes 12128256 | tf_op jit(solution)/shard_map/isd,dc->isc/dot_general | solution.py:49
  221.0 26.7 %fusion.57 = bf16[8,297,768]{2,1,0:T(8,128)(2,1)} fusion(f32[8,297,768]{2,1,0:T(8,128)} %fusion.82, f32[768]{0:T(1024)S(1)} %copy-done.51, bf16[8,297,768]{2,1,0:T(8,128)(2,1)} %all-gather.18.cloned.1.call-done, bf16[768,768]{1,0:T(8,128)(2,1)S(1)} %dynamic_update_slice.31, bf16[768,768]{1,0:T(8,128)(2,1)S(1)} %copy-done.50), kind=kOutput, calls=%fused_computation.89 | convolution fusion | flops 5744369664 | bytes 16960512 | tf_op jit(solution)/shard_map/isf,df->isd/dot_general | solution.py:80
  248.0 15.8 %all-gather.12.cloned.1.call-done = bf16[768,768]{1,0:T(8,128)(2,1)} async-done(((bf16[96,768]{1,0:T(8,128)(2,1)}), bf16[768,768]{1,0:T(8,128)(2,1)}) %all-gather.12.cloned.1.call-update) | async-done | bytes 1179664 | tf_op jit(solution)/shard_map/all_gather | solution.py:143
  263.7 10.2 %fusion.70 = (u8[297,768]{1,0:T(8,128)(4,1)S(1)}, u8[297,768]{1,0:T(8,128)(4,1)S(1)}, f32[8,297,768]{2,1,0:T(8,128)}) fusion(f32[768]{0:T(1024)S(1)} %copy-done.51, bf16[8,297,768]{2,1,0:T(8,128)(2,1)} %all-gather.10.cloned.1.call-done, bf16[768,768]{1,0:T(8,128)(2,1)} %all-gather.12.cloned.1.call-done), kind=kOutput, calls=%fused_computation.109 | convolution fusion | flops 2827934208 | bytes 12587520 | tf_op jit(solution)/shard_map/isd,dc->isc/dot_general | solution.py:49
  273.9 31.8 %all-gather.14.cloned.1.call-done = bf16[768,768]{0,1:T(8,128)(2,1)} async-done(((bf16[768,96]{0,1:T(8,128)(2,1)}), bf16[768,768]{0,1:T(8,128)(2,1)}) %all-gather.14.cloned.1.call-update) | async-done | bytes 1179664 | tf_op jit(solution)/shard_map/all_gather | solution.py:144
  305.8 23.0 %fusion.60 = bf16[8,297,768]{2,1,0:T(8,128)(2,1)} fusion(f32[8,297,768]{2,1,0:T(8,128)} %get-tuple-element.33, f32[768]{0:T(1024)S(1)} %copy-done.51, bf16[768,768]{0,1:T(8,128)(2,1)} %all-gather.14.cloned.1.call-done, u8[297,768]{1,0:T(8,128)(4,1)S(1)} %get-tuple-element.20, u8[297,768]{1,0:T(8,128)(4,1)S(1)} %get-tuple-element.19), kind=kOutput, calls=%fused_computation.90 | convolution fusion | flops 2934226944 | bytes 12587520 | tf_op jit(solution)/shard_map/isd,dc->isc/dot_general | solution.py:49
  330.6 1.9 multiply_reduce_fusion.2
  333.5 36.7 %reduce-scatter.7.cloned.1.call-done = bf16[2,297,768]{2,1,0:T(8,128)(2,1)} async-done(((bf16[8,297,768]{2,1,0:T(8,128)(2,1)}), bf16[2,297,768]{2,1,0:T(8,128)(2,1)}) %reduce-scatter.7.cloned.1.call-update) | async-done | bytes 912400 | tf_op jit(solution)/shard_map/reduce_scatter | solution.py:170
  370.2 3.6 fusion.164
  374.1 28.5 %all_gather.45 = bf16[192,768]{0,1:T(8,128)(2,1)S(1)} all-gather(bf16[192,96]{0,1:T(8,128)(2,1)S(1)} %copy.58), channel_id=1, replica_groups=mesh['dp'=8,'head'=4] {'dp'}, dimensions={1}, use_global_device_ids=true | all-gather | bytes 331776 | tf_op jit(solution)/shard_map/all_gather | solution.py:178
  402.6 39.4 %all_gather.43 = bf16[3,768,192]{2,0,1:T(4,128)(2,1)S(1)} all-gather(bf16[3,96,192]{2,0,1:T(4,128)(2,1)S(1)} %copy.56), channel_id=1, replica_groups=mesh['dp'=8,'head'=4] {'dp'}, dimensions={1}, use_global_device_ids=true | all-gather | bytes 995328 | tf_op jit(solution)/shard_map/all_gather | solution.py:177
  442.0 7.7 %convert_bitcast_fusion = bf16[3,8,297,192]{2,3,1,0:T(8,128)(2,1)S(1)} fusion(bf16[8,297,768]{2,1,0:T(8,128)(2,1)} %all-gather.8.cloned.1.call-done, bf16[3,768,192,1]{2,0,1,3:T(4,128)(2,1)S(1)} %bitcast.101), kind=kOutput, calls=%fused_computation.84 | convolution fusion | flops 2103501312 | bytes 7271424 | tf_op jit(solution)/shard_map/isd,tdc->tisc/dot_general | solution.py:55
  449.8 1.9 fusion.166
  451.7 8.2 %fusion.169 = (f32[8,3,297]{2,1,0:T(4,128)S(1)}, f32[8,3,297,297]{2,3,1,0:T(8,128)}) fusion(pred[8,297]{1,0:T(8,128)(4,1)S(1)} %copy-done.48, bf16[8,297,3,64]{1,3,2,0:T(8,128)(2,1)} %bitcast.98, bf16[8,297,3,64]{1,3,2,0:T(8,128)(2,1)} %bitcast.96), kind=kOutput, calls=%fused_computation.223 | convolution fusion | flops 279446432 | bytes 10323720 | tf_op jit(solution)/shard_map/sub | solution.py:64
  459.9 3.6 convolution_convert_fusion.1
  463.6 6.3 fusion.74
  470.1 5.2 multiply_reduce_fusion
  475.3 5.8 multiply_convert_fusion
  481.1 2.0 multiply_convert_fusion.1
  484.5 5.5 bitcast_convert_fusion
  490.1 42.3 %reduce-scatter.11.cloned.1.call-done = bf16[2,297,768]{2,1,0:T(8,128)(2,1)} async-done(((bf16[8,297,768]{2,1,0:T(8,128)(2,1)}), bf16[2,297,768]{2,1,0:T(8,128)(2,1)}) %reduce-scatter.11.cloned.1.call-update) | async-done | bytes 912400 | tf_op jit(solution)/shard_map/reduce_scatter | solution.py:205
  534.3 1.9 fusion.92
  540.0 2.8 copy.67
  545.5 122.2 %all-reduce.2.cloned.1.call-done = f32[100,768]{1,0:T(8,128)} async-done(((f32[100,768]{1,0:T(8,128)}), f32[100,768]{1,0:T(8,128)}) %all-reduce.2.cloned.1.call-update) | async-done | bytes 307216 | tf_op jit(solution)/shard_map/psum | solution.py:210
  (191 shorter events, 36.4 us)
Async XLA Ops:
  8.0 4.2 copy-start.33
  8.0 4.2 copy-start.44
  8.0 73.7 %all-gather.8.cloned.1.call-start = ((), (), s32[]{:S(2)}) async-start(), calls=%async_computation.4 | async-start | bytes 4669440 | tf_op jit(solution)/shard_map/all_gather | solution.py:155
  9.2 144.5 %copy-start = (f32[2,197,768]{2,1,0:T(8,128)}, f32[2,197,768]{2,1,0:T(8,128)S(1)}, u32[]{:S(2)}) copy-start(f32[2,197,768]{2,1,0:T(8,128)S(1)} %copy_convert_fusion) | copy-start | bytes 3631108
  10.4 143.3 %copy-start.2 = (f32[2,100,768]{2,1,0:T(8,128)}, f32[2,100,768]{2,1,0:T(8,128)S(1)}, u32[]{:S(2)}) copy-start(f32[2,100,768]{2,1,0:T(8,128)S(1)} %broadcast_in_dim.28) | copy-start | bytes 1843204
  13.6 68.1 %copy-start.43 = (s32[8,297]{1,0:T(8,128)S(1)}, s32[8,297]{1,0:T(8,128)}, u32[]{:S(2)}) copy-start(s32[8,297]{1,0:T(8,128)} %param.19) | copy-start | bytes 28516
  13.6 68.1 %copy-start.49 = (s32[8]{0:T(128)S(1)}, s32[8]{0:T(128)}, u32[]{:S(2)}) copy-start(s32[8]{0:T(128)} %param.18) | copy-start | bytes 100
  13.6 136.1 %reduce-scatter.5.cloned.1.call-start = ((), (), s32[]{:S(2)}) async-start(), calls=%async_computation.5 | async-start | bytes 4669440 | tf_op jit(solution)/shard_map/reduce_scatter | solution.py:159
  81.7 7.1 %copy-start.47 = (pred[8,297]{1,0:T(8,128)(4,1)}, pred[8,297]{1,0:T(8,128)(4,1)S(1)}, u32[]{:S(2)}) copy-start(pred[8,297]{1,0:T(8,128)(4,1)S(1)} %get-tuple-element.30) | copy-start | bytes 7132
  105.7 44.1 %copy-start.21 = (f32[768]{0:T(1024)S(1)}, f32[768]{0:T(1024)}, u32[]{:S(2)}) copy-start(f32[768]{0:T(1024)} %param.24) | copy-start | bytes 9220
  105.7 105.6 %all-gather.16.cloned.1.call-start = ((), (), s32[]{:S(2)}) async-start(), calls=%async_computation.10 | async-start | bytes 1327104 | tf_op jit(solution)/shard_map/all_gather | solution.py:179
  107.9 46.4 %copy-start.29 = (f32[768]{0:T(1024)S(1)}, f32[768]{0:T(1024)}, u32[]{:S(2)}) copy-start(f32[768]{0:T(1024)} %param.25) | copy-start | bytes 9220
  107.9 46.4 %copy-start.45 = (f32[768]{0:T(1024)S(1)}, f32[768]{0:T(1024)}, u32[]{:S(2)}) copy-start(f32[768]{0:T(1024)} %param.26) | copy-start | bytes 9220
  107.9 103.5 %all-gather.10.cloned.1.call-start = ((), (), s32[]{:S(2)}) async-start(), calls=%async_computation.6 | async-start | bytes 4669440 | tf_op jit(solution)/shard_map/all_gather | solution.py:167
  149.7 4.6 copy-start.4
  154.3 5.0 copy-start.17
  154.3 34.7 %copy-start.18 = (bf16[768,96]{0,1:T(8,128)(2,1)S(1)}, bf16[768,96]{0,1:T(8,128)(2,1)}, u32[]{:S(2)}) copy-start(bf16[768,96]{0,1:T(8,128)(2,1)} %param.29) | copy-start | bytes 442372
  155.8 65.1 %all-gather.18.cloned.1.call-start = ((), (), s32[]{:S(2)}) async-start(), calls=%async_computation.11 | async-start | bytes 4669440 | tf_op jit(solution)/shard_map/all_gather | solution.py:184
  158.5 105.2 %all-gather.12.cloned.1.call-start = ((), (), s32[]{:S(2)}) async-start(), calls=%async_computation.7 | async-start | bytes 1327104 | tf_op jit(solution)/shard_map/all_gather | solution.py:143
  159.2 146.6 %all-gather.14.cloned.1.call-start = ((), (), s32[]{:S(2)}) async-start(), calls=%async_computation.8 | async-start | bytes 1327104 | tf_op jit(solution)/shard_map/all_gather | solution.py:144
  159.3 8.7 %collective-permute-start = (bf16[768,96]{0,1:T(8,128)(2,1)S(1)}, bf16[768,96]{0,1:T(8,128)(2,1)S(1)}, u32[]{:S(2)}, u32[]{:S(2)}) collective-permute-start(bf16[768,96]{0,1:T(8,128)(2,1)S(1)} %copy-done.17), channel_id=1, source_target_pairs={{0,4},{4,8},{8,12},{12,16},{16,20},{20,24},{24,28},{28,0},{1,5},{5... | collective-permute-start | bytes 442376 | tf_op jit(solution)/shard_map/ppermute | solution.py:21
  160.8 9.8 %collective-permute-start.1 = (bf16[768,96]{0,1:T(8,128)(2,1)S(1)}, bf16[768,96]{0,1:T(8,128)(2,1)S(1)}, u32[]{:S(2)}, u32[]{:S(2)}) collective-permute-start(bf16[768,96]{0,1:T(8,128)(2,1)S(1)} %copy-done.17), channel_id=1, source_target_pairs={{0,28},{4,0},{8,4},{12,8},{16,12},{20,16},{24,20},{28,24},{1,29},{... | collective-permute-start | bytes 442376 | tf_op jit(solution)/shard_map/ppermute | solution.py:26
  168.0 9.1 %collective-permute-start.2 = (bf16[768,96]{0,1:T(8,128)(2,1)S(1)}, bf16[768,96]{0,1:T(8,128)(2,1)S(1)}, u32[]{:S(2)}, u32[]{:S(2)}) collective-permute-start(bf16[768,96]{0,1:T(8,128)(2,1)S(1)} %collective-permute-done), channel_id=1, source_target_pairs={{0,4},{4,8},{8,12},{12,16},{16,20},{20,24},{24,28},{28,0},{1,5},{5... | collective-permute-start | bytes 442376 | tf_op jit(solution)/shard_map/ppermute | solution.py:21
  170.6 9.0 %collective-permute-start.3 = (bf16[768,96]{0,1:T(8,128)(2,1)S(1)}, bf16[768,96]{0,1:T(8,128)(2,1)S(1)}, u32[]{:S(2)}, u32[]{:S(2)}) collective-permute-start(bf16[768,96]{0,1:T(8,128)(2,1)S(1)} %collective-permute-done.1), channel_id=1, source_target_pairs={{0,28},{4,0},{8,4},{12,8},{16,12},{20,16},{24,20},{28,24},{1,29},{... | collective-permute-start | bytes 442376 | tf_op jit(solution)/shard_map/ppermute | solution.py:26
  177.1 9.2 %collective-permute-start.4 = (bf16[768,96]{0,1:T(8,128)(2,1)S(1)}, bf16[768,96]{0,1:T(8,128)(2,1)S(1)}, u32[]{:S(2)}, u32[]{:S(2)}) collective-permute-start(bf16[768,96]{0,1:T(8,128)(2,1)S(1)} %collective-permute-done.2), channel_id=1, source_target_pairs={{0,4},{4,8},{8,12},{12,16},{16,20},{20,24},{24,28},{28,0},{1,5},{5... | collective-permute-start | bytes 442376 | tf_op jit(solution)/shard_map/ppermute | solution.py:21
  179.5 25.7 %collective-permute-start.5 = (bf16[768,96]{0,1:T(8,128)(2,1)S(1)}, bf16[768,96]{0,1:T(8,128)(2,1)S(1)}, u32[]{:S(2)}, u32[]{:S(2)}) collective-permute-start(bf16[768,96]{0,1:T(8,128)(2,1)S(1)} %collective-permute-done.3), channel_id=1, source_target_pairs={{0,28},{4,0},{8,4},{12,8},{16,12},{20,16},{24,20},{28,24},{1,29},{... | collective-permute-start | bytes 442376 | tf_op jit(solution)/shard_map/ppermute | solution.py:26
  186.3 22.0 %collective-permute-start.6 = (bf16[768,96]{0,1:T(8,128)(2,1)S(1)}, bf16[768,96]{0,1:T(8,128)(2,1)S(1)}, u32[]{:S(2)}, u32[]{:S(2)}) collective-permute-start(bf16[768,96]{0,1:T(8,128)(2,1)S(1)} %collective-permute-done.4), channel_id=1, source_target_pairs={{0,4},{4,8},{8,12},{12,16},{16,20},{20,24},{24,28},{28,0},{1,5},{5... | collective-permute-start | bytes 442376 | tf_op jit(solution)/shard_map/ppermute | solution.py:21
  188.8 140.2 %reduce-scatter.9.cloned.1.call-start = ((), (), s32[]{:S(2)}) async-start(), calls=%async_computation.12 | async-start | bytes 4669440 | tf_op jit(solution)/shard_map/reduce_scatter | solution.py:188
  211.3 9.7 %copy-start.51 = (f32[768]{0:T(1024)S(1)}, f32[768]{0:T(1024)}, u32[]{:S(2)}) copy-start(f32[768]{0:T(1024)} %param.28) | copy-start | bytes 9220
  211.3 9.6 %copy-start.50 = (bf16[768,768]{1,0:T(8,128)(2,1)S(1)}, bf16[768,768]{1,0:T(8,128)(2,1)}, u32[]{:S(2)}) copy-start(bf16[768,768]{1,0:T(8,128)(2,1)} %all-gather.16.cloned.1.call-done) | copy-start | bytes 3538948
  247.7 122.5 %reduce-scatter.7.cloned.1.call-start = ((), (), s32[]{:S(2)}) async-start(), calls=%async_computation.9 | async-start | bytes 4669440 | tf_op jit(solution)/shard_map/reduce_scatter | solution.py:170
  328.9 41.3 %copy-start.38 = (f32[2,297]{1,0:T(2,128)S(1)}, f32[2,297]{1,0:T(2,128)}, u32[]{:S(2)}) copy-start(f32[2,297]{1,0:T(2,128)} %copy-done.37) | copy-start | bytes 7132
  328.9 41.3 %copy-start.46 = (f32[768]{0:T(1024)S(1)}, f32[768]{0:T(1024)}, u32[]{:S(2)}) copy-start(f32[768]{0:T(1024)} %param.30) | copy-start | bytes 9220
  328.9 131.0 %all-gather.20.cloned.1.call-start = ((), (), s32[]{:S(2)}) async-start(), calls=%async_computation.13 | async-start | bytes 4669440 | tf_op jit(solution)/shard_map/all_gather | solution.py:197
  333.5 40.4 %copy-start.24 = (bf16[192,96]{1,0:T(8,128)(2,1)S(1)}, bf16[192,96]{1,0:T(8,128)(2,1)}, u32[]{:S(2)}) copy-start(bf16[192,96]{1,0:T(8,128)(2,1)} %param.23) | copy-start | bytes 110596
  333.5 40.5 %copy-start.20 = (bf16[3,96,192]{2,1,0:T(8,128)(2,1)S(1)}, bf16[3,96,192]{2,1,0:T(8,128)(2,1)}, u32[]{:S(2)}) copy-start(bf16[3,96,192]{2,1,0:T(8,128)(2,1)} %param.22) | copy-start | bytes 331780
  373.8 158.6 %reduce-scatter.11.cloned.1.call-start = ((), (), s32[]{:S(2)}) async-start(), calls=%async_computation.14 | async-start | bytes 4669440 | tf_op jit(solution)/shard_map/reduce_scatter | solution.py:205
  442.0 7.7 %copy-start.13 = (bf16[3,768,192]{2,0,1:T(4,128)(2,1)}, bf16[3,768,192]{2,0,1:T(4,128)(2,1)S(1)}, u32[]{:S(2)}) copy-start(bf16[3,768,192]{2,0,1:T(4,128)(2,1)S(1)} %all_gather.43) | copy-start | bytes 2654212
  459.9 10.0 %slice-start = ((s8[11206656]{0:T(1024)(128)(4,1)}), s8[4194304]{0:T(1024)(128)(4,1)S(1)}, s32[]{:S(2)}) async-start(s8[11206656]{0:T(1024)(128)(4,1)} %bitcast.94), calls=%async_computation.16 | async-start | bytes 8388608
  463.6 6.3 slice-start.1
  463.6 6.3 slice-start.2
  463.6 6.5 copy-start.15
  475.3 5.8 copy-start.12
  490.0 42.4 %copy-start.28 = (f32[2,297]{1,0:T(2,128)S(1)}, f32[2,297]{1,0:T(2,128)}, u32[]{:S(2)}) copy-start(f32[2,297]{1,0:T(2,128)} %copy-done.27) | copy-start | bytes 7132
  490.0 42.4 %copy-start.34 = (f32[768]{0:T(1024)S(1)}, f32[768]{0:T(1024)}, u32[]{:S(2)}) copy-start(f32[768]{0:T(1024)} %param.20) | copy-start | bytes 9220
  490.0 44.3 %copy-start.40 = (f32[2,297]{1,0:T(2,128)S(1)}, f32[2,297]{1,0:T(2,128)}, u32[]{:S(2)}) copy-start(f32[2,297]{1,0:T(2,128)} %copy-done.39) | copy-start | bytes 7132
  490.0 44.3 %copy-start.36 = (f32[2,297]{1,0:T(2,128)S(1)}, f32[2,297]{1,0:T(2,128)}, u32[]{:S(2)}) copy-start(f32[2,297]{1,0:T(2,128)} %copy-done.35) | copy-start | bytes 7132
  490.0 177.7 %all-reduce.2.cloned.1.call-start = ((), (), s32[]{:S(2)}) async-start(), calls=%async_computation.15 | async-start | bytes 638976 | tf_op jit(solution)/shard_map/psum | solution.py:210
  (26 other events, 53.9 us)
Sparse Core Ops, SparseCore 0:
  13.7 33.0 all-gather.7
  105.8 43.8 reduce-scatter.4
  247.8 41.6 reduce-scatter.8
  329.0 41.1 reduce-scatter.6
  540.1 127.4 all-reduce.1
Sparse Core Ops, SparseCore 1:
  108.6 42.6 all-gather.15
  155.9 31.7 all-gather.9
  189.2 31.7 all-gather.17
  223.2 40.5 all-gather.11
  266.0 39.8 all-gather.13
  373.9 31.7 all-gather.19
  490.1 42.2 reduce-scatter.10
